TPU v7x, 32 devices: a whole 2x2x4 slice. The times are simulated.
32 devices in a mesh: gx: 4 (over z), gy: 4 (over y, core), gz: 2 (over x).
Axes of the slice: x: 2, y: 2, z: 4, core: 2. Of those that a mesh axis runs over, the one named last changes fastest.
Arguments:
- load: bfloat16 [4, 4, 2, 64, 1152], P('gx', 'gy', 'gz'), may hold values from -6 to 6
- schur: bfloat16 [4, 4, 2, 1152, 1152], P('gx', 'gy', 'gz')
- neumann: bfloat16 [4, 4, 2, 6, 192, 192], P('gx', 'gy', 'gz')
- coarse_basis: bfloat16 [4, 4, 2, 8, 1152], P('gx', 'gy', 'gz'), may hold values from -5 to 5
- coarse_rows: bfloat16 [4, 4, 2, 8, 256], P('gx', 'gy', 'gz'), may hold values from -0.0078125 to 0.0078125
Outputs:
- iterate: bfloat16 [4, 4, 2, 64, 1152], P('gx', 'gy', 'gz')
All inputs are finite; a program needn't handle non-finite values.
Results may differ from a plain program's by a relative error of at most 0.0048.
Values sent between devices are 32-bit elements; how exact they have to be, the bound alone decides.
No kernel may reach another device: no remote copies, remote signals or barrier semaphores. Data moves between devices by JAX's collectives and lax.ppermute only.
A program may use at most 64 MiB of HBM per device.

v0:
```python
import jax
import jax.numpy as jnp
from jax import lax
from jax.sharding import PartitionSpec as P

ITERS = 2


def padded_2(shard, sides, width):
    for axis, dim in sides:
        devices, length = (lax.axis_size(axis), shard.shape[dim])
        up = [(i, (i + 1) % devices) for i in range(devices - 1)]
        down = [(j, i) for i, j in up]
        last = lax.slice_in_dim(shard, length - width, length, axis=dim)
        initial = lax.slice_in_dim(shard, 0, width, axis=dim)
        before = lax.ppermute(last, axis, up)
        after = lax.ppermute(initial, axis, down)
        shard = jnp.concatenate([before, shard, after], axis=dim)
    return shard


def x_faces(vec):
    padded = padded_2(vec[:, 0:2], (("gx", 1),), 1)
    return [padded[:, 0], padded[:, 3]]


def y_faces(vec):
    padded = padded_2(vec[:, 2:4], (("gy", 1),), 1)
    return [padded[:, 0], padded[:, 3]]


def z_faces(vec):
    padded = padded_2(vec[:, 4:6], (("gz", 1),), 1)
    return [padded[:, 0], padded[:, 3]]


def assemble(vec):
    pieces = x_faces(vec) + y_faces(vec) + z_faces(vec)
    return vec + jnp.stack(pieces, axis=1)


def side_weights(place, extent):
    lower = jnp.where(place > 0, 0.5, 1.0).astype(jnp.float32)
    upper = jnp.where(place < extent - 1, 0.5, 1.0).astype(jnp.float32)
    return [lower, upper]


def face_weights():
    values = side_weights(lax.axis_index("gx"), lax.axis_size("gx"))
    values = values + side_weights(lax.axis_index("gy"), lax.axis_size("gy"))
    values = values + side_weights(lax.axis_index("gz"), lax.axis_size("gz"))
    return jnp.stack(values).reshape(1, 6, 1)


def contract_rows(whole, rows_f):
    return lax.dot_general(whole, rows_f, (((1,), (1,)), ((), ())), precision=lax.Precision.HIGHEST)


def coarse_solve(coarse_in, rows_f):
    column = lax.all_gather(coarse_in, "gz", axis=1, tiled=True)
    whole = lax.all_gather(column, ("gx", "gy"), axis=1, tiled=True)
    return contract_rows(whole, rows_f)


def body(load, schur, neumann, coarse_basis, coarse_rows):
    count = load.shape[3]
    width = load.shape[4]
    face = width // 6
    load_f = load.reshape(count, width).astype(jnp.float32)
    schur_m = schur.reshape(width, width)
    blocks = neumann.reshape(6, face, face)
    basis = coarse_basis.reshape(coarse_basis.shape[3], width)
    basis_f = basis.astype(jnp.float32)
    rows_f = coarse_rows.reshape(coarse_rows.shape[3], coarse_rows.shape[4]).astype(jnp.float32)
    weight = face_weights()
    iterate = jnp.zeros((count, width), jnp.float32)
    for step in range(ITERS):
        if step == 0:
            local = load_f
        else:
            local = load_f - jnp.dot(
                iterate.astype(jnp.bfloat16), schur_m, preferred_element_type=jnp.float32
            )
        resid = assemble(local.reshape(count, 6, face))
        scaled = (resid * weight).astype(jnp.bfloat16)
        flat = scaled.reshape(count, width)
        coarse_in = lax.dot_general(
            flat, basis, (((1,), (1,)), ((), ())), preferred_element_type=jnp.float32
        )
        coarse_out = coarse_solve(coarse_in, rows_f)
        local_part = jnp.einsum("rfa,fab->rfb", scaled, blocks, preferred_element_type=jnp.float32)
        coarse_part = jnp.dot(coarse_out, basis_f, precision=lax.Precision.HIGHEST)
        correction = local_part + coarse_part.reshape(count, 6, face)
        update = assemble(correction * weight)
        iterate = iterate + 0.5 * update.reshape(count, width)
    return iterate.astype(jnp.bfloat16).reshape(load.shape)


def solution(mesh):
    placed = (
        P("gx", "gy", "gz", None, None),
        P("gx", "gy", "gz", None, None),
        P("gx", "gy", "gz", None, None, None),
        P("gx", "gy", "gz", None, None),
        P("gx", "gy", "gz", None, None),
    )
    return jax.shard_map(
        body, mesh=mesh, in_specs=placed, out_specs=P("gx", "gy", "gz", None, None), check_vma=False
    )
```

profile of v0, /device:TPU:0, one launch (start us, length us, event | category | flops | bytes accessed | tf_op | source)
XLA Modules:
  0.0 143.1 jit_solution(15394782454922018203)
XLA Ops:
  2.1 5.6 %collective-permute-start = (f32[64,1,192]{2,0,1:T(8,128)}, f32[64,1,192]{2,0,1:T(8,128)}, u32[]{:S(2)}, u32[]{:S(2)}) collective-permute-start(f32[64,1,192]{2,0,1:T(8,128)} %get-tuple-element.30), channel_id=1, source_target_pairs={{0,8},{8,16},{16,24},{1,9},{9,17},{17,25},{2,10},{10,18},{18,26},{... | collective-permute-start | bytes 147464 | tf_op jit(solution)/shard_map/ppermute | solution.py:16
  9.0 2.1 %collective-permute-start.2 = (f32[64,1,192]{2,0,1:T(8,128)S(1)}, f32[64,1,192]{2,0,1:T(8,128)}, u32[]{:S(2)}, u32[]{:S(2)}) collective-permute-start(f32[64,1,192]{2,0,1:T(8,128)S(1)} %get-tuple-element.28), channel_id=1, source_target_pairs={{0,2},{2,4},{4,6},{1,3},{3,5},{5,7},{8,10},{10,12},{12,14},{9,11},... | collective-permute-start | bytes 147464 | tf_op jit(solution)/shard_map/ppermute | solution.py:16
  12.3 4.0 %collective-permute-start.4 = (f32[64,1,192]{2,0,1:T(8,128)S(1)}, f32[64,1,192]{2,0,1:T(8,128)}, u32[]{:S(2)}, u32[]{:S(2)}) collective-permute-start(f32[64,1,192]{2,0,1:T(8,128)S(1)} %get-tuple-element.26), channel_id=1, source_target_pairs={{0,1},{2,3},{4,5},{6,7},{8,9},{10,11},{12,13},{14,15},{16,17},{18,... | collective-permute-start | bytes 147464 | tf_op jit(solution)/shard_map/ppermute | solution.py:16
  17.3 1.4 collective-permute-start.5
  24.4 4.4 %all_gather.12 = f32[64,16]{0,1:T(8,128)S(1)} all-gather(f32[64,8]{0,1:T(8,128)S(1)} %fusion.13), channel_id=1, replica_groups=mesh['gx'=4,'gy'=4,'gz'=2] {'gz'}, dimensions={1}, use_global_device_ids=true | all-gather | bytes 6144 | tf_op jit(solution)/shard_map/all_gather | solution.py:60
  28.8 25.3 %all_gather.13 = f32[64,256]{0,1:T(8,128)S(1)} all-gather(f32[64,16]{0,1:T(8,128)S(1)} %all_gather.12), channel_id=1, replica_groups=mesh['gx'=4,'gy'=4,'gz'=2] {'gx','gy'}, dimensions={1}, use_global_device_ids=true | all-gather | bytes 69632 | tf_op jit(solution)/shard_map/all_gather | solution.py:61
  54.6 1.3 collective-permute-start.6
  57.2 2.3 %collective-permute-start.8 = (f32[64,1,192]{2,0,1:T(8,128)S(1)}, f32[64,1,192]{2,0,1:T(8,128)S(1)}, u32[]{:S(2)}, u32[]{:S(2)}) collective-permute-start(f32[64,1,192]{2,0,1:T(8,128)S(1)} %get-tuple-element.22), channel_id=1, source_target_pairs={{0,2},{2,4},{4,6},{1,3},{3,5},{5,7},{8,10},{10,12},{12,14},{9,11},... | collective-permute-start | bytes 147464 | tf_op jit(solution)/shard_map/ppermute | solution.py:16
  60.8 3.9 %collective-permute-start.10 = (f32[64,1,192]{2,0,1:T(8,128)S(1)}, f32[64,1,192]{2,0,1:T(8,128)S(1)}, u32[]{:S(2)}, u32[]{:S(2)}) collective-permute-start(f32[64,1,192]{2,0,1:T(8,128)S(1)} %get-tuple-element.20), channel_id=1, source_target_pairs={{0,1},{2,3},{4,5},{6,7},{8,9},{10,11},{12,13},{14,15},{16,17},{18,... | collective-permute-start | bytes 147464 | tf_op jit(solution)/shard_map/ppermute | solution.py:16
  67.1 4.4 %collective-permute-done.11 = f32[64,1,192]{2,0,1:T(8,128)S(1)} collective-permute-done((f32[64,1,192]{2,0,1:T(8,128)S(1)}, f32[64,1,192]{2,0,1:T(8,128)S(1)}, u32[]{:S(2)}, u32[]{:S(2)}) %collective-permute-start.11) | collective-permute-done | bytes 49184 | tf_op jit(solution)/shard_map/ppermute | solution.py:17
  76.1 4.9 %collective-permute-start.12 = (f32[64,1,192]{2,0,1:T(8,128)}, f32[64,1,192]{2,0,1:T(8,128)}, u32[]{:S(2)}, u32[]{:S(2)}) collective-permute-start(f32[64,1,192]{2,0,1:T(8,128)} %get-tuple-element.18), channel_id=1, source_target_pairs={{0,8},{8,16},{16,24},{1,9},{9,17},{17,25},{2,10},{10,18},{18,26},{... | collective-permute-start | bytes 147464 | tf_op jit(solution)/shard_map/ppermute | solution.py:16
  82.4 1.6 %collective-permute-start.14 = (f32[64,1,192]{2,0,1:T(8,128)}, f32[64,1,192]{2,0,1:T(8,128)S(1)}, u32[]{:S(2)}, u32[]{:S(2)}) collective-permute-start(f32[64,1,192]{2,0,1:T(8,128)} %get-tuple-element.16), channel_id=1, source_target_pairs={{0,2},{2,4},{4,6},{1,3},{3,5},{5,7},{8,10},{10,12},{12,14},{9,11},... | collective-permute-start | bytes 147464 | tf_op jit(solution)/shard_map/ppermute | solution.py:16
  85.3 1.5 %collective-permute-start.16 = (f32[64,1,192]{2,0,1:T(8,128)S(1)}, f32[64,1,192]{2,0,1:T(8,128)S(1)}, u32[]{:S(2)}, u32[]{:S(2)}) collective-permute-start(f32[64,1,192]{2,0,1:T(8,128)S(1)} %get-tuple-element.14), channel_id=1, source_target_pairs={{0,1},{2,3},{4,5},{6,7},{8,9},{10,11},{12,13},{14,15},{16,17},{18,... | collective-permute-start | bytes 147464 | tf_op jit(solution)/shard_map/ppermute | solution.py:16
  86.8 1.3 collective-permute-start.17
  89.0 3.9 %collective-permute-done.17 = f32[64,1,192]{2,0,1:T(8,128)S(1)} collective-permute-done((f32[64,1,192]{2,0,1:T(8,128)S(1)}, f32[64,1,192]{2,0,1:T(8,128)S(1)}, u32[]{:S(2)}, u32[]{:S(2)}) %collective-permute-start.17) | collective-permute-done | bytes 49184 | tf_op jit(solution)/shard_map/ppermute | solution.py:17
  93.0 2.1 %convolution_bitcast_fusion = f32[64,6,192]{2,0,1:T(8,128)} fusion(bf16[1,1,1,6,192,192]{5,4,3,2,1,0:T(8,128)(2,1)} %param.7, f32[64,6,192]{2,0,1:T(8,128)S(1)} %copy.44, f32[64,6,192]{2,0,1:T(8,128)S(1)} %constant_dynamic-update-slice_fusion.12, f32[6]{0:T(128)S(1)} %stack.42), kind=kOutput, calls=%fused_computation.5 | convolution fusion | flops 28532736 | bytes 1327128 | tf_op jit(solution)/shard_map/rfa,fab->rfb/dot_general | solution.py:91
  97.3 4.4 %all_gather.14 = f32[64,16]{0,1:T(8,128)S(1)} all-gather(f32[64,8]{0,1:T(8,128)S(1)} %fusion.10), channel_id=1, replica_groups=mesh['gx'=4,'gy'=4,'gz'=2] {'gz'}, dimensions={1}, use_global_device_ids=true | all-gather | bytes 6144 | tf_op jit(solution)/shard_map/all_gather | solution.py:60
  101.7 23.9 %all_gather.15 = f32[64,256]{0,1:T(8,128)S(1)} all-gather(f32[64,16]{0,1:T(8,128)S(1)} %all_gather.14), channel_id=1, replica_groups=mesh['gx'=4,'gy'=4,'gz'=2] {'gx','gy'}, dimensions={1}, use_global_device_ids=true | all-gather | bytes 69632 | tf_op jit(solution)/shard_map/all_gather | solution.py:61
  125.8 1.4 fusion.5
  127.2 1.3 collective-permute-start.18
  128.5 1.3 collective-permute-start.19
  129.8 2.2 %collective-permute-start.20 = (f32[64,1,192]{2,0,1:T(8,128)S(1)}, f32[64,1,192]{2,0,1:T(8,128)S(1)}, u32[]{:S(2)}, u32[]{:S(2)}) collective-permute-start(f32[64,1,192]{2,0,1:T(8,128)S(1)} %get-tuple-element.10), channel_id=1, source_target_pairs={{0,2},{2,4},{4,6},{1,3},{3,5},{5,7},{8,10},{10,12},{12,14},{9,11},... | collective-permute-start | bytes 147464 | tf_op jit(solution)/shard_map/ppermute | solution.py:16
  133.4 1.9 %collective-permute-start.22 = (f32[64,1,192]{2,0,1:T(8,128)S(1)}, f32[64,1,192]{2,0,1:T(8,128)S(1)}, u32[]{:S(2)}, u32[]{:S(2)}) collective-permute-start(f32[64,1,192]{2,0,1:T(8,128)S(1)} %get-tuple-element.8), channel_id=1, source_target_pairs={{0,1},{2,3},{4,5},{6,7},{8,9},{10,11},{12,13},{14,15},{16,17},{18,... | collective-permute-start | bytes 147464 | tf_op jit(solution)/shard_map/ppermute | solution.py:16
  137.6 4.4 %collective-permute-done.23 = f32[64,1,192]{2,0,1:T(8,128)S(1)} collective-permute-done((f32[64,1,192]{2,0,1:T(8,128)S(1)}, f32[64,1,192]{2,0,1:T(8,128)S(1)}, u32[]{:S(2)}, u32[]{:S(2)}) %collective-permute-start.23) | collective-permute-done | bytes 49184 | tf_op jit(solution)/shard_map/ppermute | solution.py:17
  (96 shorter events, 31.8 us)
Async XLA Ops:
  2.1 15.2 %collective-permute-start = (f32[64,1,192]{2,0,1:T(8,128)}, f32[64,1,192]{2,0,1:T(8,128)}, u32[]{:S(2)}, u32[]{:S(2)}) collective-permute-start(f32[64,1,192]{2,0,1:T(8,128)} %get-tuple-element.30), channel_id=1, source_target_pairs={{0,8},{8,16},{16,24},{1,9},{9,17},{17,25},{2,10},{10,18},{18,26},{... | collective-permute-start | bytes 147464 | tf_op jit(solution)/shard_map/ppermute | solution.py:16
  7.7 11.9 %collective-permute-start.1 = (f32[64,1,192]{2,0,1:T(8,128)}, f32[64,1,192]{2,0,1:T(8,128)}, u32[]{:S(2)}, u32[]{:S(2)}) collective-permute-start(f32[64,1,192]{2,0,1:T(8,128)} %get-tuple-element.29), channel_id=1, source_target_pairs={{8,0},{16,8},{24,16},{9,1},{17,9},{25,17},{10,2},{18,10},{26,18},{... | collective-permute-start | bytes 147464 | tf_op jit(solution)/shard_map/ppermute | solution.py:17
  9.0 11.4 %collective-permute-start.2 = (f32[64,1,192]{2,0,1:T(8,128)S(1)}, f32[64,1,192]{2,0,1:T(8,128)}, u32[]{:S(2)}, u32[]{:S(2)}) collective-permute-start(f32[64,1,192]{2,0,1:T(8,128)S(1)} %get-tuple-element.28), channel_id=1, source_target_pairs={{0,2},{2,4},{4,6},{1,3},{3,5},{5,7},{8,10},{10,12},{12,14},{9,11},... | collective-permute-start | bytes 147464 | tf_op jit(solution)/shard_map/ppermute | solution.py:16
  11.0 10.2 %collective-permute-start.3 = (f32[64,1,192]{2,0,1:T(8,128)S(1)}, f32[64,1,192]{2,0,1:T(8,128)}, u32[]{:S(2)}, u32[]{:S(2)}) collective-permute-start(f32[64,1,192]{2,0,1:T(8,128)S(1)} %get-tuple-element.27), channel_id=1, source_target_pairs={{2,0},{4,2},{6,4},{3,1},{5,3},{7,5},{10,8},{12,10},{14,12},{11,9},... | collective-permute-start | bytes 147464 | tf_op jit(solution)/shard_map/ppermute | solution.py:17
  12.3 9.8 %collective-permute-start.4 = (f32[64,1,192]{2,0,1:T(8,128)S(1)}, f32[64,1,192]{2,0,1:T(8,128)}, u32[]{:S(2)}, u32[]{:S(2)}) collective-permute-start(f32[64,1,192]{2,0,1:T(8,128)S(1)} %get-tuple-element.26), channel_id=1, source_target_pairs={{0,1},{2,3},{4,5},{6,7},{8,9},{10,11},{12,13},{14,15},{16,17},{18,... | collective-permute-start | bytes 147464 | tf_op jit(solution)/shard_map/ppermute | solution.py:16
  17.3 6.3 %collective-permute-start.5 = (f32[64,1,192]{2,0,1:T(8,128)S(1)}, f32[64,1,192]{2,0,1:T(8,128)S(1)}, u32[]{:S(2)}, u32[]{:S(2)}) collective-permute-start(f32[64,1,192]{2,0,1:T(8,128)S(1)} %get-tuple-element.25), channel_id=1, source_target_pairs={{1,0},{3,2},{5,4},{7,6},{9,8},{11,10},{13,12},{15,14},{17,16},{19,... | collective-permute-start | bytes 147464 | tf_op jit(solution)/shard_map/ppermute | solution.py:17
  54.6 10.1 %collective-permute-start.6 = (f32[64,1,192]{2,0,1:T(8,128)S(1)}, f32[64,1,192]{2,0,1:T(8,128)S(1)}, u32[]{:S(2)}, u32[]{:S(2)}) collective-permute-start(f32[64,1,192]{2,0,1:T(8,128)S(1)} %get-tuple-element.24), channel_id=1, source_target_pairs={{0,8},{8,16},{16,24},{1,9},{9,17},{17,25},{2,10},{10,18},{18,26},{... | collective-permute-start | bytes 147464 | tf_op jit(solution)/shard_map/ppermute | solution.py:16
  55.9 10.1 %collective-permute-start.7 = (f32[64,1,192]{2,0,1:T(8,128)S(1)}, f32[64,1,192]{2,0,1:T(8,128)S(1)}, u32[]{:S(2)}, u32[]{:S(2)}) collective-permute-start(f32[64,1,192]{2,0,1:T(8,128)S(1)} %get-tuple-element.23), channel_id=1, source_target_pairs={{8,0},{16,8},{24,16},{9,1},{17,9},{25,17},{10,2},{18,10},{26,18},{... | collective-permute-start | bytes 147464 | tf_op jit(solution)/shard_map/ppermute | solution.py:17
  57.2 8.9 %collective-permute-start.8 = (f32[64,1,192]{2,0,1:T(8,128)S(1)}, f32[64,1,192]{2,0,1:T(8,128)S(1)}, u32[]{:S(2)}, u32[]{:S(2)}) collective-permute-start(f32[64,1,192]{2,0,1:T(8,128)S(1)} %get-tuple-element.22), channel_id=1, source_target_pairs={{0,2},{2,4},{4,6},{1,3},{3,5},{5,7},{8,10},{10,12},{12,14},{9,11},... | collective-permute-start | bytes 147464 | tf_op jit(solution)/shard_map/ppermute | solution.py:16
  59.5 6.6 %collective-permute-start.9 = (f32[64,1,192]{2,0,1:T(8,128)S(1)}, f32[64,1,192]{2,0,1:T(8,128)S(1)}, u32[]{:S(2)}, u32[]{:S(2)}) collective-permute-start(f32[64,1,192]{2,0,1:T(8,128)S(1)} %get-tuple-element.21), channel_id=1, source_target_pairs={{2,0},{4,2},{6,4},{3,1},{5,3},{7,5},{10,8},{12,10},{14,12},{11,9},... | collective-permute-start | bytes 147464 | tf_op jit(solution)/shard_map/ppermute | solution.py:17
  60.8 6.3 %collective-permute-start.10 = (f32[64,1,192]{2,0,1:T(8,128)S(1)}, f32[64,1,192]{2,0,1:T(8,128)S(1)}, u32[]{:S(2)}, u32[]{:S(2)}) collective-permute-start(f32[64,1,192]{2,0,1:T(8,128)S(1)} %get-tuple-element.20), channel_id=1, source_target_pairs={{0,1},{2,3},{4,5},{6,7},{8,9},{10,11},{12,13},{14,15},{16,17},{18,... | collective-permute-start | bytes 147464 | tf_op jit(solution)/shard_map/ppermute | solution.py:16
  64.8 6.7 %collective-permute-start.11 = (f32[64,1,192]{2,0,1:T(8,128)S(1)}, f32[64,1,192]{2,0,1:T(8,128)S(1)}, u32[]{:S(2)}, u32[]{:S(2)}) collective-permute-start(f32[64,1,192]{2,0,1:T(8,128)S(1)} %get-tuple-element.19), channel_id=1, source_target_pairs={{1,0},{3,2},{5,4},{7,6},{9,8},{11,10},{13,12},{15,14},{17,16},{19,... | collective-permute-start | bytes 147464 | tf_op jit(solution)/shard_map/ppermute | solution.py:17
  76.1 10.7 %collective-permute-start.12 = (f32[64,1,192]{2,0,1:T(8,128)}, f32[64,1,192]{2,0,1:T(8,128)}, u32[]{:S(2)}, u32[]{:S(2)}) collective-permute-start(f32[64,1,192]{2,0,1:T(8,128)} %get-tuple-element.18), channel_id=1, source_target_pairs={{0,8},{8,16},{16,24},{1,9},{9,17},{17,25},{2,10},{10,18},{18,26},{... | collective-permute-start | bytes 147464 | tf_op jit(solution)/shard_map/ppermute | solution.py:16
  81.1 7.8 %collective-permute-start.13 = (f32[64,1,192]{2,0,1:T(8,128)}, f32[64,1,192]{2,0,1:T(8,128)S(1)}, u32[]{:S(2)}, u32[]{:S(2)}) collective-permute-start(f32[64,1,192]{2,0,1:T(8,128)} %get-tuple-element.17), channel_id=1, source_target_pairs={{8,0},{16,8},{24,16},{9,1},{17,9},{25,17},{10,2},{18,10},{26,18},{... | collective-permute-start | bytes 147464 | tf_op jit(solution)/shard_map/ppermute | solution.py:17
  82.4 6.6 %collective-permute-start.14 = (f32[64,1,192]{2,0,1:T(8,128)}, f32[64,1,192]{2,0,1:T(8,128)S(1)}, u32[]{:S(2)}, u32[]{:S(2)}) collective-permute-start(f32[64,1,192]{2,0,1:T(8,128)} %get-tuple-element.16), channel_id=1, source_target_pairs={{0,2},{2,4},{4,6},{1,3},{3,5},{5,7},{8,10},{10,12},{12,14},{9,11},... | collective-permute-start | bytes 147464 | tf_op jit(solution)/shard_map/ppermute | solution.py:16
  84.0 5.0 %collective-permute-start.15 = (f32[64,1,192]{2,0,1:T(8,128)}, f32[64,1,192]{2,0,1:T(8,128)S(1)}, u32[]{:S(2)}, u32[]{:S(2)}) collective-permute-start(f32[64,1,192]{2,0,1:T(8,128)} %get-tuple-element.15), channel_id=1, source_target_pairs={{2,0},{4,2},{6,4},{3,1},{5,3},{7,5},{10,8},{12,10},{14,12},{11,9},... | collective-permute-start | bytes 147464 | tf_op jit(solution)/shard_map/ppermute | solution.py:17
  85.3 3.7 %collective-permute-start.16 = (f32[64,1,192]{2,0,1:T(8,128)S(1)}, f32[64,1,192]{2,0,1:T(8,128)S(1)}, u32[]{:S(2)}, u32[]{:S(2)}) collective-permute-start(f32[64,1,192]{2,0,1:T(8,128)S(1)} %get-tuple-element.14), channel_id=1, source_target_pairs={{0,1},{2,3},{4,5},{6,7},{8,9},{10,11},{12,13},{14,15},{16,17},{18,... | collective-permute-start | bytes 147464 | tf_op jit(solution)/shard_map/ppermute | solution.py:16
  86.8 6.2 %collective-permute-start.17 = (f32[64,1,192]{2,0,1:T(8,128)S(1)}, f32[64,1,192]{2,0,1:T(8,128)S(1)}, u32[]{:S(2)}, u32[]{:S(2)}) collective-permute-start(f32[64,1,192]{2,0,1:T(8,128)S(1)} %get-tuple-element.13), channel_id=1, source_target_pairs={{1,0},{3,2},{5,4},{7,6},{9,8},{11,10},{13,12},{15,14},{17,16},{19,... | collective-permute-start | bytes 147464 | tf_op jit(solution)/shard_map/ppermute | solution.py:17
  127.2 8.1 %collective-permute-start.18 = (f32[64,1,192]{2,0,1:T(8,128)S(1)}, f32[64,1,192]{2,0,1:T(8,128)S(1)}, u32[]{:S(2)}, u32[]{:S(2)}) collective-permute-start(f32[64,1,192]{2,0,1:T(8,128)S(1)} %get-tuple-element.12), channel_id=1, source_target_pairs={{0,8},{8,16},{16,24},{1,9},{9,17},{17,25},{2,10},{10,18},{18,26},{... | collective-permute-start | bytes 147464 | tf_op jit(solution)/shard_map/ppermute | solution.py:16
  128.5 8.1 %collective-permute-start.19 = (f32[64,1,192]{2,0,1:T(8,128)S(1)}, f32[64,1,192]{2,0,1:T(8,128)S(1)}, u32[]{:S(2)}, u32[]{:S(2)}) collective-permute-start(f32[64,1,192]{2,0,1:T(8,128)S(1)} %get-tuple-element.11), channel_id=1, source_target_pairs={{8,0},{16,8},{24,16},{9,1},{17,9},{25,17},{10,2},{18,10},{26,18},{... | collective-permute-start | bytes 147464 | tf_op jit(solution)/shard_map/ppermute | solution.py:17
  129.8 6.8 %collective-permute-start.20 = (f32[64,1,192]{2,0,1:T(8,128)S(1)}, f32[64,1,192]{2,0,1:T(8,128)S(1)}, u32[]{:S(2)}, u32[]{:S(2)}) collective-permute-start(f32[64,1,192]{2,0,1:T(8,128)S(1)} %get-tuple-element.10), channel_id=1, source_target_pairs={{0,2},{2,4},{4,6},{1,3},{3,5},{5,7},{8,10},{10,12},{12,14},{9,11},... | collective-permute-start | bytes 147464 | tf_op jit(solution)/shard_map/ppermute | solution.py:16
  132.1 4.6 %collective-permute-start.21 = (f32[64,1,192]{2,0,1:T(8,128)S(1)}, f32[64,1,192]{2,0,1:T(8,128)S(1)}, u32[]{:S(2)}, u32[]{:S(2)}) collective-permute-start(f32[64,1,192]{2,0,1:T(8,128)S(1)} %get-tuple-element.9), channel_id=1, source_target_pairs={{2,0},{4,2},{6,4},{3,1},{5,3},{7,5},{10,8},{12,10},{14,12},{11,9},... | collective-permute-start | bytes 147464 | tf_op jit(solution)/shard_map/ppermute | solution.py:17
  133.4 4.2 %collective-permute-start.22 = (f32[64,1,192]{2,0,1:T(8,128)S(1)}, f32[64,1,192]{2,0,1:T(8,128)S(1)}, u32[]{:S(2)}, u32[]{:S(2)}) collective-permute-start(f32[64,1,192]{2,0,1:T(8,128)S(1)} %get-tuple-element.8), channel_id=1, source_target_pairs={{0,1},{2,3},{4,5},{6,7},{8,9},{10,11},{12,13},{14,15},{16,17},{18,... | collective-permute-start | bytes 147464 | tf_op jit(solution)/shard_map/ppermute | solution.py:16
  135.3 6.7 %collective-permute-start.23 = (f32[64,1,192]{2,0,1:T(8,128)S(1)}, f32[64,1,192]{2,0,1:T(8,128)S(1)}, u32[]{:S(2)}, u32[]{:S(2)}) collective-permute-start(f32[64,1,192]{2,0,1:T(8,128)S(1)} %get-tuple-element.7), channel_id=1, source_target_pairs={{1,0},{3,2},{5,4},{7,6},{9,8},{11,10},{13,12},{15,14},{17,16},{19,... | collective-permute-start | bytes 147464 | tf_op jit(solution)/shard_map/ppermute | solution.py:17
  (6 other events, 248.9 us)
where the time goes:
time: 144 us; the launch traced here: 143 us
  blocking collectives  58 us (40%)
  starting transfers between devices  48.1 us (33%)
  waiting for transfers between devices  15.3 us (11%)
  local copies, waits for them, and re-layouts  13.9 us (10%)
  matrix products  6.25 us (4%)
    all_gather x2, blocking collectives, coarse_solve(): whole = lax.all_gather(column, ('gx', 'gy'), axis=1, tiled=True)  49.2 us
    ppermute x12, starting transfers between devices, padded_2(): before = lax.ppermute(last, axis, up)  32.5 us
    ppermute x12, starting transfers between devices, padded_2(): after = lax.ppermute(initial, axis, down)  15.6 us
    ppermute x12, waiting for transfers between devices, padded_2(): after = lax.ppermute(initial, axis, down)  13.4 us
    all_gather x2, blocking collectives, coarse_solve(): column = lax.all_gather(coarse_in, 'gz', axis=1, tiled=True)  8.77 us
    unnamed x32, local copies, waits for them, and re-layouts  5.19 us
  transfers between devices with their start and end apart: 24, of which 6 were waited for; matrix products, arithmetic and copies ran while one was open for 4% of the time, Pallas kernels for 0%

commit v1 on v0

--- a/solution.py
+++ b/solution.py
@@ -57,7 +57,7 @@
 
 
 def coarse_solve(coarse_in, rows_f):
-    column = lax.all_gather(coarse_in, "gz", axis=1, tiled=True)
+    column = jnp.concatenate(lax.all_gather(coarse_in, "gz"), axis=1)
     whole = lax.all_gather(column, ("gx", "gy"), axis=1, tiled=True)
     return contract_rows(whole, rows_f)
 

time: 144 us -> 144 us (level)
  no operation moved by 1% of the time
where the time goes in v1:
time: 144 us; the launch traced here: 143 us
  blocking collectives  58 us (40%)
  starting transfers between devices  48.1 us (33%)
  waiting for transfers between devices  15.3 us (11%)
  local copies, waits for them, and re-layouts  13.9 us (10%)
  matrix products  6.25 us (4%)
    all_gather x2, blocking collectives, coarse_solve(): whole = lax.all_gather(column, ('gx', 'gy'), axis=1, tiled=True)  49.2 us
    ppermute x12, starting transfers between devices, padded_2(): before = lax.ppermute(last, axis, up)  32.5 us
    ppermute x12, starting transfers between devices, padded_2(): after = lax.ppermute(initial, axis, down)  15.6 us
    ppermute x12, waiting for transfers between devices, padded_2(): after = lax.ppermute(initial, axis, down)  13.4 us
    all_gather x2, blocking collectives, coarse_solve(): column = jnp.concatenate(lax.all_gather(coarse_in, 'gz'), axis=1)  8.77 us
    unnamed x32, local copies, waits for them, and re-layouts  5.19 us
  transfers between devices with their start and end apart: 24, of which 6 were waited for; matrix products, arithmetic and copies ran while one was open for 4% of the time, Pallas kernels for 0%

profile of v1, /device:TPU:0, one launch (start us, length us, event | category | flops | bytes accessed | tf_op | source)
XLA Modules:
  0.0 143.1 jit_solution(7194089165420671859)
XLA Ops:
  2.1 5.6 %collective-permute-start = (f32[64,1,192]{2,0,1:T(8,128)}, f32[64,1,192]{2,0,1:T(8,128)}, u32[]{:S(2)}, u32[]{:S(2)}) collective-permute-start(f32[64,1,192]{2,0,1:T(8,128)} %get-tuple-element.30), channel_id=1, source_target_pairs={{0,8},{8,16},{16,24},{1,9},{9,17},{17,25},{2,10},{10,18},{18,26},{... | collective-permute-start | bytes 147464 | tf_op jit(solution)/shard_map/ppermute | solution.py:16
  9.0 2.1 %collective-permute-start.2 = (f32[64,1,192]{2,0,1:T(8,128)S(1)}, f32[64,1,192]{2,0,1:T(8,128)}, u32[]{:S(2)}, u32[]{:S(2)}) collective-permute-start(f32[64,1,192]{2,0,1:T(8,128)S(1)} %get-tuple-element.28), channel_id=1, source_target_pairs={{0,2},{2,4},{4,6},{1,3},{3,5},{5,7},{8,10},{10,12},{12,14},{9,11},... | collective-permute-start | bytes 147464 | tf_op jit(solution)/shard_map/ppermute | solution.py:16
  12.3 4.0 %collective-permute-start.4 = (f32[64,1,192]{2,0,1:T(8,128)S(1)}, f32[64,1,192]{2,0,1:T(8,128)}, u32[]{:S(2)}, u32[]{:S(2)}) collective-permute-start(f32[64,1,192]{2,0,1:T(8,128)S(1)} %get-tuple-element.26), channel_id=1, source_target_pairs={{0,1},{2,3},{4,5},{6,7},{8,9},{10,11},{12,13},{14,15},{16,17},{18,... | collective-permute-start | bytes 147464 | tf_op jit(solution)/shard_map/ppermute | solution.py:16
  17.3 1.4 collective-permute-start.5
  24.4 4.4 %all-gather.2 = f32[2,64,8]{1,2,0:T(8,128)S(1)} all-gather(f32[1,64,8]{1,2,0:T(8,128)S(1)} %convolution_bitcast_fusion.5), channel_id=2, replica_groups=mesh['gx'=4,'gy'=4,'gz'=2] {'gz'}, dimensions={0}, use_global_device_ids=true | all-gather | bytes 6144 | tf_op jit(solution)/shard_map/all_gather | solution.py:60
  28.8 25.3 %all_gather.20 = f32[64,256]{0,1:T(8,128)S(1)} all-gather(f32[64,16]{0,1:T(8,128)S(1)} %bitcast.60), channel_id=1, replica_groups=mesh['gx'=4,'gy'=4,'gz'=2] {'gx','gy'}, dimensions={1}, use_global_device_ids=true | all-gather | bytes 69632 | tf_op jit(solution)/shard_map/all_gather | solution.py:61
  54.6 1.3 collective-permute-start.6
  57.2 2.3 %collective-permute-start.8 = (f32[64,1,192]{2,0,1:T(8,128)S(1)}, f32[64,1,192]{2,0,1:T(8,128)S(1)}, u32[]{:S(2)}, u32[]{:S(2)}) collective-permute-start(f32[64,1,192]{2,0,1:T(8,128)S(1)} %get-tuple-element.22), channel_id=1, source_target_pairs={{0,2},{2,4},{4,6},{1,3},{3,5},{5,7},{8,10},{10,12},{12,14},{9,11},... | collective-permute-start | bytes 147464 | tf_op jit(solution)/shard_map/ppermute | solution.py:16
  60.8 3.9 %collective-permute-start.10 = (f32[64,1,192]{2,0,1:T(8,128)S(1)}, f32[64,1,192]{2,0,1:T(8,128)S(1)}, u32[]{:S(2)}, u32[]{:S(2)}) collective-permute-start(f32[64,1,192]{2,0,1:T(8,128)S(1)} %get-tuple-element.20), channel_id=1, source_target_pairs={{0,1},{2,3},{4,5},{6,7},{8,9},{10,11},{12,13},{14,15},{16,17},{18,... | collective-permute-start | bytes 147464 | tf_op jit(solution)/shard_map/ppermute | solution.py:16
  67.1 4.4 %collective-permute-done.11 = f32[64,1,192]{2,0,1:T(8,128)S(1)} collective-permute-done((f32[64,1,192]{2,0,1:T(8,128)S(1)}, f32[64,1,192]{2,0,1:T(8,128)S(1)}, u32[]{:S(2)}, u32[]{:S(2)}) %collective-permute-start.11) | collective-permute-done | bytes 49184 | tf_op jit(solution)/shard_map/ppermute | solution.py:17
  76.1 4.9 %collective-permute-start.12 = (f32[64,1,192]{2,0,1:T(8,128)}, f32[64,1,192]{2,0,1:T(8,128)}, u32[]{:S(2)}, u32[]{:S(2)}) collective-permute-start(f32[64,1,192]{2,0,1:T(8,128)} %get-tuple-element.18), channel_id=1, source_target_pairs={{0,8},{8,16},{16,24},{1,9},{9,17},{17,25},{2,10},{10,18},{18,26},{... | collective-permute-start | bytes 147464 | tf_op jit(solution)/shard_map/ppermute | solution.py:16
  82.4 1.6 %collective-permute-start.14 = (f32[64,1,192]{2,0,1:T(8,128)}, f32[64,1,192]{2,0,1:T(8,128)S(1)}, u32[]{:S(2)}, u32[]{:S(2)}) collective-permute-start(f32[64,1,192]{2,0,1:T(8,128)} %get-tuple-element.16), channel_id=1, source_target_pairs={{0,2},{2,4},{4,6},{1,3},{3,5},{5,7},{8,10},{10,12},{12,14},{9,11},... | collective-permute-start | bytes 147464 | tf_op jit(solution)/shard_map/ppermute | solution.py:16
  85.3 1.5 %collective-permute-start.16 = (f32[64,1,192]{2,0,1:T(8,128)S(1)}, f32[64,1,192]{2,0,1:T(8,128)S(1)}, u32[]{:S(2)}, u32[]{:S(2)}) collective-permute-start(f32[64,1,192]{2,0,1:T(8,128)S(1)} %get-tuple-element.14), channel_id=1, source_target_pairs={{0,1},{2,3},{4,5},{6,7},{8,9},{10,11},{12,13},{14,15},{16,17},{18,... | collective-permute-start | bytes 147464 | tf_op jit(solution)/shard_map/ppermute | solution.py:16
  86.8 1.3 collective-permute-start.17
  89.0 3.9 %collective-permute-done.17 = f32[64,1,192]{2,0,1:T(8,128)S(1)} collective-permute-done((f32[64,1,192]{2,0,1:T(8,128)S(1)}, f32[64,1,192]{2,0,1:T(8,128)S(1)}, u32[]{:S(2)}, u32[]{:S(2)}) %collective-permute-start.17) | collective-permute-done | bytes 49184 | tf_op jit(solution)/shard_map/ppermute | solution.py:17
  93.0 2.1 %convolution_bitcast_fusion = f32[64,6,192]{2,0,1:T(8,128)} fusion(bf16[1,1,1,6,192,192]{5,4,3,2,1,0:T(8,128)(2,1)} %param.7, f32[64,6,192]{2,0,1:T(8,128)S(1)} %copy.44, f32[64,6,192]{2,0,1:T(8,128)S(1)} %constant_dynamic-update-slice_fusion.12, f32[6]{0:T(128)S(1)} %stack.42), kind=kOutput, calls=%fused_computation.5 | convolution fusion | flops 28532736 | bytes 1327128 | tf_op jit(solution)/shard_map/rfa,fab->rfb/dot_general | solution.py:91
  97.3 4.4 %all-gather.3 = f32[2,64,8]{1,2,0:T(8,128)S(1)} all-gather(f32[1,64,8]{1,2,0:T(8,128)S(1)} %convolution_bitcast_fusion.3), channel_id=3, replica_groups=mesh['gx'=4,'gy'=4,'gz'=2] {'gz'}, dimensions={0}, use_global_device_ids=true | all-gather | bytes 6144 | tf_op jit(solution)/shard_map/all_gather | solution.py:60
  101.7 23.9 %all_gather.23 = f32[64,256]{0,1:T(8,128)S(1)} all-gather(f32[64,16]{0,1:T(8,128)S(1)} %bitcast.61), channel_id=1, replica_groups=mesh['gx'=4,'gy'=4,'gz'=2] {'gx','gy'}, dimensions={1}, use_global_device_ids=true | all-gather | bytes 69632 | tf_op jit(solution)/shard_map/all_gather | solution.py:61
  125.8 1.4 fusion.5
  127.2 1.3 collective-permute-start.18
  128.5 1.3 collective-permute-start.19
  129.8 2.2 %collective-permute-start.20 = (f32[64,1,192]{2,0,1:T(8,128)S(1)}, f32[64,1,192]{2,0,1:T(8,128)S(1)}, u32[]{:S(2)}, u32[]{:S(2)}) collective-permute-start(f32[64,1,192]{2,0,1:T(8,128)S(1)} %get-tuple-element.10), channel_id=1, source_target_pairs={{0,2},{2,4},{4,6},{1,3},{3,5},{5,7},{8,10},{10,12},{12,14},{9,11},... | collective-permute-start | bytes 147464 | tf_op jit(solution)/shard_map/ppermute | solution.py:16
  133.4 1.9 %collective-permute-start.22 = (f32[64,1,192]{2,0,1:T(8,128)S(1)}, f32[64,1,192]{2,0,1:T(8,128)S(1)}, u32[]{:S(2)}, u32[]{:S(2)}) collective-permute-start(f32[64,1,192]{2,0,1:T(8,128)S(1)} %get-tuple-element.8), channel_id=1, source_target_pairs={{0,1},{2,3},{4,5},{6,7},{8,9},{10,11},{12,13},{14,15},{16,17},{18,... | collective-permute-start | bytes 147464 | tf_op jit(solution)/shard_map/ppermute | solution.py:16
  137.6 4.4 %collective-permute-done.23 = f32[64,1,192]{2,0,1:T(8,128)S(1)} collective-permute-done((f32[64,1,192]{2,0,1:T(8,128)S(1)}, f32[64,1,192]{2,0,1:T(8,128)S(1)}, u32[]{:S(2)}, u32[]{:S(2)}) %collective-permute-start.23) | collective-permute-done | bytes 49184 | tf_op jit(solution)/shard_map/ppermute | solution.py:17
  (96 shorter events, 31.8 us)
Async XLA Ops:
  2.1 15.2 %collective-permute-start = (f32[64,1,192]{2,0,1:T(8,128)}, f32[64,1,192]{2,0,1:T(8,128)}, u32[]{:S(2)}, u32[]{:S(2)}) collective-permute-start(f32[64,1,192]{2,0,1:T(8,128)} %get-tuple-element.30), channel_id=1, source_target_pairs={{0,8},{8,16},{16,24},{1,9},{9,17},{17,25},{2,10},{10,18},{18,26},{... | collective-permute-start | bytes 147464 | tf_op jit(solution)/shard_map/ppermute | solution.py:16
  7.7 11.9 %collective-permute-start.1 = (f32[64,1,192]{2,0,1:T(8,128)}, f32[64,1,192]{2,0,1:T(8,128)}, u32[]{:S(2)}, u32[]{:S(2)}) collective-permute-start(f32[64,1,192]{2,0,1:T(8,128)} %get-tuple-element.29), channel_id=1, source_target_pairs={{8,0},{16,8},{24,16},{9,1},{17,9},{25,17},{10,2},{18,10},{26,18},{... | collective-permute-start | bytes 147464 | tf_op jit(solution)/shard_map/ppermute | solution.py:17
  9.0 11.4 %collective-permute-start.2 = (f32[64,1,192]{2,0,1:T(8,128)S(1)}, f32[64,1,192]{2,0,1:T(8,128)}, u32[]{:S(2)}, u32[]{:S(2)}) collective-permute-start(f32[64,1,192]{2,0,1:T(8,128)S(1)} %get-tuple-element.28), channel_id=1, source_target_pairs={{0,2},{2,4},{4,6},{1,3},{3,5},{5,7},{8,10},{10,12},{12,14},{9,11},... | collective-permute-start | bytes 147464 | tf_op jit(solution)/shard_map/ppermute | solution.py:16
  11.0 10.2 %collective-permute-start.3 = (f32[64,1,192]{2,0,1:T(8,128)S(1)}, f32[64,1,192]{2,0,1:T(8,128)}, u32[]{:S(2)}, u32[]{:S(2)}) collective-permute-start(f32[64,1,192]{2,0,1:T(8,128)S(1)} %get-tuple-element.27), channel_id=1, source_target_pairs={{2,0},{4,2},{6,4},{3,1},{5,3},{7,5},{10,8},{12,10},{14,12},{11,9},... | collective-permute-start | bytes 147464 | tf_op jit(solution)/shard_map/ppermute | solution.py:17
  12.3 9.8 %collective-permute-start.4 = (f32[64,1,192]{2,0,1:T(8,128)S(1)}, f32[64,1,192]{2,0,1:T(8,128)}, u32[]{:S(2)}, u32[]{:S(2)}) collective-permute-start(f32[64,1,192]{2,0,1:T(8,128)S(1)} %get-tuple-element.26), channel_id=1, source_target_pairs={{0,1},{2,3},{4,5},{6,7},{8,9},{10,11},{12,13},{14,15},{16,17},{18,... | collective-permute-start | bytes 147464 | tf_op jit(solution)/shard_map/ppermute | solution.py:16
  17.3 6.3 %collective-permute-start.5 = (f32[64,1,192]{2,0,1:T(8,128)S(1)}, f32[64,1,192]{2,0,1:T(8,128)S(1)}, u32[]{:S(2)}, u32[]{:S(2)}) collective-permute-start(f32[64,1,192]{2,0,1:T(8,128)S(1)} %get-tuple-element.25), channel_id=1, source_target_pairs={{1,0},{3,2},{5,4},{7,6},{9,8},{11,10},{13,12},{15,14},{17,16},{19,... | collective-permute-start | bytes 147464 | tf_op jit(solution)/shard_map/ppermute | solution.py:17
  54.6 10.1 %collective-permute-start.6 = (f32[64,1,192]{2,0,1:T(8,128)S(1)}, f32[64,1,192]{2,0,1:T(8,128)S(1)}, u32[]{:S(2)}, u32[]{:S(2)}) collective-permute-start(f32[64,1,192]{2,0,1:T(8,128)S(1)} %get-tuple-element.24), channel_id=1, source_target_pairs={{0,8},{8,16},{16,24},{1,9},{9,17},{17,25},{2,10},{10,18},{18,26},{... | collective-permute-start | bytes 147464 | tf_op jit(solution)/shard_map/ppermute | solution.py:16
  55.9 10.1 %collective-permute-start.7 = (f32[64,1,192]{2,0,1:T(8,128)S(1)}, f32[64,1,192]{2,0,1:T(8,128)S(1)}, u32[]{:S(2)}, u32[]{:S(2)}) collective-permute-start(f32[64,1,192]{2,0,1:T(8,128)S(1)} %get-tuple-element.23), channel_id=1, source_target_pairs={{8,0},{16,8},{24,16},{9,1},{17,9},{25,17},{10,2},{18,10},{26,18},{... | collective-permute-start | bytes 147464 | tf_op jit(solution)/shard_map/ppermute | solution.py:17
  57.2 8.9 %collective-permute-start.8 = (f32[64,1,192]{2,0,1:T(8,128)S(1)}, f32[64,1,192]{2,0,1:T(8,128)S(1)}, u32[]{:S(2)}, u32[]{:S(2)}) collective-permute-start(f32[64,1,192]{2,0,1:T(8,128)S(1)} %get-tuple-element.22), channel_id=1, source_target_pairs={{0,2},{2,4},{4,6},{1,3},{3,5},{5,7},{8,10},{10,12},{12,14},{9,11},... | collective-permute-start | bytes 147464 | tf_op jit(solution)/shard_map/ppermute | solution.py:16
  59.5 6.6 %collective-permute-start.9 = (f32[64,1,192]{2,0,1:T(8,128)S(1)}, f32[64,1,192]{2,0,1:T(8,128)S(1)}, u32[]{:S(2)}, u32[]{:S(2)}) collective-permute-start(f32[64,1,192]{2,0,1:T(8,128)S(1)} %get-tuple-element.21), channel_id=1, source_target_pairs={{2,0},{4,2},{6,4},{3,1},{5,3},{7,5},{10,8},{12,10},{14,12},{11,9},... | collective-permute-start | bytes 147464 | tf_op jit(solution)/shard_map/ppermute | solution.py:17
  60.8 6.3 %collective-permute-start.10 = (f32[64,1,192]{2,0,1:T(8,128)S(1)}, f32[64,1,192]{2,0,1:T(8,128)S(1)}, u32[]{:S(2)}, u32[]{:S(2)}) collective-permute-start(f32[64,1,192]{2,0,1:T(8,128)S(1)} %get-tuple-element.20), channel_id=1, source_target_pairs={{0,1},{2,3},{4,5},{6,7},{8,9},{10,11},{12,13},{14,15},{16,17},{18,... | collective-permute-start | bytes 147464 | tf_op jit(solution)/shard_map/ppermute | solution.py:16
  64.8 6.7 %collective-permute-start.11 = (f32[64,1,192]{2,0,1:T(8,128)S(1)}, f32[64,1,192]{2,0,1:T(8,128)S(1)}, u32[]{:S(2)}, u32[]{:S(2)}) collective-permute-start(f32[64,1,192]{2,0,1:T(8,128)S(1)} %get-tuple-element.19), channel_id=1, source_target_pairs={{1,0},{3,2},{5,4},{7,6},{9,8},{11,10},{13,12},{15,14},{17,16},{19,... | collective-permute-start | bytes 147464 | tf_op jit(solution)/shard_map/ppermute | solution.py:17
  76.1 10.7 %collective-permute-start.12 = (f32[64,1,192]{2,0,1:T(8,128)}, f32[64,1,192]{2,0,1:T(8,128)}, u32[]{:S(2)}, u32[]{:S(2)}) collective-permute-start(f32[64,1,192]{2,0,1:T(8,128)} %get-tuple-element.18), channel_id=1, source_target_pairs={{0,8},{8,16},{16,24},{1,9},{9,17},{17,25},{2,10},{10,18},{18,26},{... | collective-permute-start | bytes 147464 | tf_op jit(solution)/shard_map/ppermute | solution.py:16
  81.1 7.8 %collective-permute-start.13 = (f32[64,1,192]{2,0,1:T(8,128)}, f32[64,1,192]{2,0,1:T(8,128)S(1)}, u32[]{:S(2)}, u32[]{:S(2)}) collective-permute-start(f32[64,1,192]{2,0,1:T(8,128)} %get-tuple-element.17), channel_id=1, source_target_pairs={{8,0},{16,8},{24,16},{9,1},{17,9},{25,17},{10,2},{18,10},{26,18},{... | collective-permute-start | bytes 147464 | tf_op jit(solution)/shard_map/ppermute | solution.py:17
  82.4 6.6 %collective-permute-start.14 = (f32[64,1,192]{2,0,1:T(8,128)}, f32[64,1,192]{2,0,1:T(8,128)S(1)}, u32[]{:S(2)}, u32[]{:S(2)}) collective-permute-start(f32[64,1,192]{2,0,1:T(8,128)} %get-tuple-element.16), channel_id=1, source_target_pairs={{0,2},{2,4},{4,6},{1,3},{3,5},{5,7},{8,10},{10,12},{12,14},{9,11},... | collective-permute-start | bytes 147464 | tf_op jit(solution)/shard_map/ppermute | solution.py:16
  84.0 5.0 %collective-permute-start.15 = (f32[64,1,192]{2,0,1:T(8,128)}, f32[64,1,192]{2,0,1:T(8,128)S(1)}, u32[]{:S(2)}, u32[]{:S(2)}) collective-permute-start(f32[64,1,192]{2,0,1:T(8,128)} %get-tuple-element.15), channel_id=1, source_target_pairs={{2,0},{4,2},{6,4},{3,1},{5,3},{7,5},{10,8},{12,10},{14,12},{11,9},... | collective-permute-start | bytes 147464 | tf_op jit(solution)/shard_map/ppermute | solution.py:17
  85.3 3.7 %collective-permute-start.16 = (f32[64,1,192]{2,0,1:T(8,128)S(1)}, f32[64,1,192]{2,0,1:T(8,128)S(1)}, u32[]{:S(2)}, u32[]{:S(2)}) collective-permute-start(f32[64,1,192]{2,0,1:T(8,128)S(1)} %get-tuple-element.14), channel_id=1, source_target_pairs={{0,1},{2,3},{4,5},{6,7},{8,9},{10,11},{12,13},{14,15},{16,17},{18,... | collective-permute-start | bytes 147464 | tf_op jit(solution)/shard_map/ppermute | solution.py:16
  86.8 6.2 %collective-permute-start.17 = (f32[64,1,192]{2,0,1:T(8,128)S(1)}, f32[64,1,192]{2,0,1:T(8,128)S(1)}, u32[]{:S(2)}, u32[]{:S(2)}) collective-permute-start(f32[64,1,192]{2,0,1:T(8,128)S(1)} %get-tuple-element.13), channel_id=1, source_target_pairs={{1,0},{3,2},{5,4},{7,6},{9,8},{11,10},{13,12},{15,14},{17,16},{19,... | collective-permute-start | bytes 147464 | tf_op jit(solution)/shard_map/ppermute | solution.py:17
  127.2 8.1 %collective-permute-start.18 = (f32[64,1,192]{2,0,1:T(8,128)S(1)}, f32[64,1,192]{2,0,1:T(8,128)S(1)}, u32[]{:S(2)}, u32[]{:S(2)}) collective-permute-start(f32[64,1,192]{2,0,1:T(8,128)S(1)} %get-tuple-element.12), channel_id=1, source_target_pairs={{0,8},{8,16},{16,24},{1,9},{9,17},{17,25},{2,10},{10,18},{18,26},{... | collective-permute-start | bytes 147464 | tf_op jit(solution)/shard_map/ppermute | solution.py:16
  128.5 8.1 %collective-permute-start.19 = (f32[64,1,192]{2,0,1:T(8,128)S(1)}, f32[64,1,192]{2,0,1:T(8,128)S(1)}, u32[]{:S(2)}, u32[]{:S(2)}) collective-permute-start(f32[64,1,192]{2,0,1:T(8,128)S(1)} %get-tuple-element.11), channel_id=1, source_target_pairs={{8,0},{16,8},{24,16},{9,1},{17,9},{25,17},{10,2},{18,10},{26,18},{... | collective-permute-start | bytes 147464 | tf_op jit(solution)/shard_map/ppermute | solution.py:17
  129.8 6.8 %collective-permute-start.20 = (f32[64,1,192]{2,0,1:T(8,128)S(1)}, f32[64,1,192]{2,0,1:T(8,128)S(1)}, u32[]{:S(2)}, u32[]{:S(2)}) collective-permute-start(f32[64,1,192]{2,0,1:T(8,128)S(1)} %get-tuple-element.10), channel_id=1, source_target_pairs={{0,2},{2,4},{4,6},{1,3},{3,5},{5,7},{8,10},{10,12},{12,14},{9,11},... | collective-permute-start | bytes 147464 | tf_op jit(solution)/shard_map/ppermute | solution.py:16
  132.1 4.6 %collective-permute-start.21 = (f32[64,1,192]{2,0,1:T(8,128)S(1)}, f32[64,1,192]{2,0,1:T(8,128)S(1)}, u32[]{:S(2)}, u32[]{:S(2)}) collective-permute-start(f32[64,1,192]{2,0,1:T(8,128)S(1)} %get-tuple-element.9), channel_id=1, source_target_pairs={{2,0},{4,2},{6,4},{3,1},{5,3},{7,5},{10,8},{12,10},{14,12},{11,9},... | collective-permute-start | bytes 147464 | tf_op jit(solution)/shard_map/ppermute | solution.py:17
  133.4 4.2 %collective-permute-start.22 = (f32[64,1,192]{2,0,1:T(8,128)S(1)}, f32[64,1,192]{2,0,1:T(8,128)S(1)}, u32[]{:S(2)}, u32[]{:S(2)}) collective-permute-start(f32[64,1,192]{2,0,1:T(8,128)S(1)} %get-tuple-element.8), channel_id=1, source_target_pairs={{0,1},{2,3},{4,5},{6,7},{8,9},{10,11},{12,13},{14,15},{16,17},{18,... | collective-permute-start | bytes 147464 | tf_op jit(solution)/shard_map/ppermute | solution.py:16
  135.3 6.7 %collective-permute-start.23 = (f32[64,1,192]{2,0,1:T(8,128)S(1)}, f32[64,1,192]{2,0,1:T(8,128)S(1)}, u32[]{:S(2)}, u32[]{:S(2)}) collective-permute-start(f32[64,1,192]{2,0,1:T(8,128)S(1)} %get-tuple-element.7), channel_id=1, source_target_pairs={{1,0},{3,2},{5,4},{7,6},{9,8},{11,10},{13,12},{15,14},{17,16},{19,... | collective-permute-start | bytes 147464 | tf_op jit(solution)/shard_map/ppermute | solution.py:17
  (6 other events, 248.9 us)
